TPU v7x, 128 devices: a whole 4x4x4 slice. The times are simulated.
128 devices in a mesh: ctx: 16 (over x, z_hi, core), tp: 8 (over y, z_lo).
Axes of the slice: x: 4, y: 4, z: 4 (z_hi: 2, z_lo: 2; z = z_hi * 2 + z_lo), core: 2. Of those that a mesh axis runs over, the one named last changes fastest.
Arguments:
- query_proj: bfloat16 [6144, 4096], P('ctx', 'tp'), may hold values from -6 to 6
- key_proj: bfloat16 [6144, 4096], P('ctx', 'tp'), may hold values from -6 to 6
- value_proj: bfloat16 [6144, 4096], P('ctx', 'tp'), may hold values from -6 to 6
- saved_conv: bfloat16 [6144, 4096], P('ctx', 'tp'), may hold values from -6 to 6
- grad_out: bfloat16 [6144, 4096], P(('ctx', 'tp')), may hold values from -6 to 6
- filters: bfloat16 [256, 6144], P('tp'), may hold values from -0.109375 to 0.109375
- featurizer: float32 [3, 3, 4096], P(None, None, 'tp'), may hold values from -2 to 2
Outputs:
- grad_query: bfloat16 [6144, 4096], P('ctx', 'tp')
- grad_key: bfloat16 [6144, 4096], P('ctx', 'tp')
- grad_value: bfloat16 [6144, 4096], P('ctx', 'tp')
All inputs are finite; a program needn't handle non-finite values.
Results may differ from a plain program's by a relative error of at most 0.012.
Values may be sent and summed in bfloat16 or wider, within the bound.
A program may use at most 256 MiB of HBM per device.

v0:
```python
import jax
import jax.numpy as jnp
from jax import lax
from jax.sharding import PartitionSpec as P

GSIZE = 16
TAPS = 3


def shifted(array, axis, by):
    length = lax.axis_size(axis)
    pairs = [(i, i + by) for i in range(length) if 0 <= i + by < length]
    return lax.ppermute(array, axis, pairs)


def featurize(current, previous, kernel):
    amount = current.shape[0]
    joined = jnp.concatenate([previous, current], axis=0).astype(jnp.float32)
    total = kernel[0] * joined[TAPS - 1 : TAPS - 1 + amount]
    for offset in range(1, TAPS):
        total = total + kernel[offset] * joined[TAPS - 1 - offset : TAPS - 1 - offset + amount]
    return total


def spread(current, following, kernel):
    amount = current.shape[0]
    joined = jnp.concatenate([current, following], axis=0)
    total = kernel[0] * joined[0:amount]
    for offset in range(1, TAPS):
        total = total + kernel[offset] * joined[offset : offset + amount]
    return total


def toeplitz_tiles(window, tile_rows, width_k):
    groups = window.shape[0]
    padded = jnp.concatenate([window, jnp.zeros((groups, 1), window.dtype)], axis=1)
    tiled = jnp.tile(padded, (1, tile_rows))
    folded = tiled[:, : tile_rows * (width_k + tile_rows - 1)].reshape(
        groups, tile_rows, width_k + tile_rows - 1
    )
    return folded[:, :, tile_rows - 1 : tile_rows - 1 + width_k]


def cross_terms(source, src_start, dst_start, dst_rows, filt_pad, front_pad, tile_rows):
    groups = filt_pad.shape[0]
    src_rows = source.shape[0]
    src_tiles = -(-src_rows // tile_rows)
    dst_tiles = dst_rows // tile_rows
    width_k = (dst_tiles + src_tiles - 1) * tile_rows
    lag_first = src_start - dst_start - (dst_tiles - 1) * tile_rows - (tile_rows - 1)
    window = lax.dynamic_slice_in_dim(filt_pad, lag_first + front_pad, width_k + tile_rows - 1, 1)
    tiles = toeplitz_tiles(window, tile_rows, width_k)
    pieces = source.reshape(src_tiles, tile_rows, groups, GSIZE)
    result = jnp.zeros((dst_tiles, tile_rows, groups, GSIZE), jnp.float32)
    for diagonal in range(dst_tiles + src_tiles - 1):
        offset = diagonal - (dst_tiles - 1)
        lowest = max(0, -offset)
        highest = min(dst_tiles, src_tiles - offset)
        matrix = tiles[:, :, diagonal * tile_rows : (diagonal + 1) * tile_rows]
        product = jnp.einsum(
            "gij,ajgc->aigc",
            matrix,
            pieces[lowest + offset : highest + offset],
            preferred_element_type=jnp.float32,
        )
        result = result.at[lowest:highest].add(product)
    return result.reshape(dst_rows, groups * GSIZE)


def body(query_proj, key_proj, value_proj, saved_conv, grad_out, filters, featurizer):
    block_rows, channels = query_proj.shape
    tokens = filters.shape[1]
    tile_rows = min(128, block_rows)
    own_start = lax.axis_index("ctx") * block_rows
    front_pad = 2 * tokens
    filt_pad = jnp.pad(filters, ((0, 0), (front_pad, tokens + 2 * tile_rows)))
    upstream = lax.all_to_all(grad_out, "tp", split_axis=1, concat_axis=0, tiled=True)
    previous = shifted(
        (
            query_proj[block_rows - (TAPS - 1) :],
            key_proj[block_rows - (TAPS - 1) :],
            value_proj[block_rows - (TAPS - 1) :],
        ),
        "ctx",
        1,
    )
    query_feat = featurize(query_proj, previous[0], featurizer[0])
    key_feat = featurize(key_proj, previous[1], featurizer[1])
    value_feat = featurize(value_proj, previous[2], featurizer[2])
    upstream_f = upstream.astype(jnp.float32)
    grad_qfeat = upstream_f * saved_conv.astype(jnp.float32)
    grad_conv = (upstream_f * query_feat).astype(jnp.bfloat16)
    empty = jnp.zeros((block_rows, channels), jnp.float32)
    piece = lax.all_gather(grad_conv, "ctx", axis=0, tiled=True)
    piece_start = jnp.int32(0)
    grad_mix = lax.cond(
        piece_start + piece.shape[0] > own_start,
        lambda: cross_terms(
            piece, piece_start, own_start, block_rows, filt_pad, front_pad, tile_rows
        ),
        lambda: empty,
    )
    grad_kfeat = grad_mix * value_feat
    grad_vfeat = grad_mix * key_feat
    following = shifted(
        (grad_qfeat[: TAPS - 1], grad_kfeat[: TAPS - 1], grad_vfeat[: TAPS - 1]), "ctx", -1
    )
    grad_query = spread(grad_qfeat, following[0], featurizer[0]).astype(jnp.bfloat16)
    grad_key = spread(grad_kfeat, following[1], featurizer[1]).astype(jnp.bfloat16)
    grad_value = spread(grad_vfeat, following[2], featurizer[2]).astype(jnp.bfloat16)
    return (grad_query, grad_key, grad_value)


def solution(mesh):
    return jax.shard_map(
        body,
        mesh=mesh,
        in_specs=(
            P("ctx", "tp"),
            P("ctx", "tp"),
            P("ctx", "tp"),
            P("ctx", "tp"),
            P(("ctx", "tp"), None),
            P("tp", None),
            P(None, None, "tp"),
        ),
        out_specs=(P("ctx", "tp"), P("ctx", "tp"), P("ctx", "tp")),
        check_vma=False,
    )
```

profile of v0, /device:TPU:1, one launch (start us, length us, event | category | flops | bytes accessed | tf_op | source)
XLA Modules:
  0.0 704.6 jit_solution(5903635782921676362)
XLA Ops:
  7.9 6.9 collective-permute-start.1
  16.5 4.6 all-to-all-start
  23.8 4.0 all-to-all-done
  30.7 5.2 collective-permute-start.2
  45.7 48.6 %all-gather.2.cloned.1.call-done = bf16[6144,512]{1,0:T(8,128)(2,1)} async-done(((bf16[384,512]{1,0:T(8,128)(2,1)}), bf16[6144,512]{1,0:T(8,128)(2,1)}) %all-gather.2.cloned.1.call-update) | async-done | bytes 6291472 | tf_op jit(solution)/shard_map/all_gather | solution.py:94
  94.4 589.0 %conditional.1 = (f32[384,512]{1,0:T(8,128)}) conditional(s32[]{:T(128)} %convert_element_type.43, () %tuple.355, (bf16[32,6144]{1,0:T(8,128)(2,1)}, s32[]{:T(128)}, bf16[6144,512]{1,0:T(8,128)(2,1)}) %tuple.356), branch_computations={%region_0.1_spmd, %region_1.2_spmd} | conditional | flops 2425290752 | bytes 657653696 | solution.py:96
  95.8 17.2 %tile.1 = bf16[32,128,6528]{2,1,0:T(8,128)(2,1)} broadcast(bf16[32,6528]{1,0:T(8,128)(2,1)S(1)} %concatenate.114), dimensions={0,2} | broadcast | bytes 53895168 | tf_op jit(solution)/shard_map/cond/branch_1_fun/tile | solution.py:37
  113.0 49.0 %copy.164 = bf16[4,8,128,6528]{3,1,2,0:T(8,128)(2,1)} copy(bf16[4,8,128,6528]{3,2,1,0:T(8,128)(2,1)} %bitcast.572) | data formatting | bytes 106954752 | tf_op jit(solution)/shard_map/cond
  162.0 35.7 %slice.1975 = bf16[32,835456]{1,0:T(8,128)(2,1)} slice(bf16[32,835584]{1,0:T(8,128)(2,1)} %bitcast.573), slice={[0:32], [0:835456]} | slice | bytes 106938368 | tf_op jit(solution)/shard_map/cond/branch_1_fun/slice | solution.py:38
  197.7 208.9 %reshape.2132 = bf16[32,128,6527]{2,1,0:T(8,128)(2,1)} reshape(bf16[32,835456]{1,0:T(8,128)(2,1)} %slice.1975) | data formatting | bytes 106938368 | tf_op jit(solution)/shard_map/cond/branch_1_fun/reshape | solution.py:38
  406.5 8.9 %copy.159 = bf16[6144,512]{0,1:T(8,128)(2,1)} copy(bf16[6144,512]{1,0:T(8,128)(2,1)} %get-tuple-element.998) | data formatting | bytes 12582912 | tf_op jit(solution)/shard_map
  416.6 2.3 fusion.97
  423.1 6.3 fusion.131
  430.9 3.4 fusion.95
  434.3 6.4 fusion.132
  442.1 3.4 fusion.49
  447.0 3.4 fusion.47
  451.9 3.4 fusion.45
  456.8 3.4 fusion.43
  461.6 3.4 fusion.41
  466.5 3.4 fusion.39
  471.8 3.4 fusion.37
  476.7 3.4 fusion.35
  481.5 3.4 fusion.33
  486.4 3.4 fusion.31
  491.3 3.4 fusion.93
  496.2 3.4 fusion.29
  501.0 3.4 fusion.27
  505.9 3.4 fusion.25
  510.8 3.4 fusion.23
  515.6 3.4 fusion.21
  520.7 3.4 fusion.19
  525.5 3.4 fusion.17
  530.4 3.4 fusion.15
  535.3 3.4 fusion.13
  540.2 3.4 fusion.11
  545.1 3.4 fusion.9
  549.9 3.4 fusion.7
  554.8 3.4 fusion.5
  559.7 3.5 fusion.75
  564.6 3.4 fusion.73
  569.7 3.4 fusion.71
  574.6 3.4 fusion.69
  579.4 3.4 fusion.67
  584.3 3.4 fusion.65
  589.2 3.4 fusion.63
  594.0 3.4 fusion.61
  598.9 3.4 fusion.59
  603.8 3.4 fusion.57
  608.7 3.4 fusion.55
  613.5 3.4 fusion.53
  618.8 3.4 fusion.51
  622.2 3.7 fusion.133
  627.4 3.4 fusion.91
  632.2 3.4 fusion.89
  637.1 3.4 fusion.87
  642.0 3.4 fusion.85
  646.9 3.4 fusion.83
  651.7 3.4 fusion.81
  656.6 3.4 fusion.79
  661.5 2.5 fusion.77
  664.0 12.7 %bitcast_add_fusion = f32[3,128,32,16]{1,3,2,0:T(8,128)S(1)} fusion(f32[3,128,32,16]{1,3,2,0:T(8,128)S(1)} %fusion.100, f32[32,128,3,16]{1,3,2,0:T(8,128)} %bitcast.600, f32[32,128,3,16]{1,3,2,0:T(8,128)} %bitcast.599, f32[32,128,3,16]{1,3,2,0:T(8,128)} %bitcast.598, f32[32,128,3,16]{1,3,2,0:T(8,128)} %bitcast.597, f32[32,128,3,16]{1,3,2,0:T(8,128)} %bitcast.596, ...), kind=kLoop, calls=%fused_computation.104 | loop fusion | flops 9043968 | bytes 37748736 | tf_op jit(solution)/shard_map/cond/branch_1_fun/add | solution.py:66
  687.4 2.8 fusion.115
  693.1 3.5 collective-permute-done.3
  (159 shorter events, 106.7 us)
Async XLA Ops:
  7.9 14.8 %collective-permute-start.1 = (bf16[2,512]{1,0:T(2,128)(2,1)S(1)}, bf16[2,512]{1,0:T(2,128)(2,1)S(1)}, u32[]{:S(2)}, u32[]{:S(2)}) collective-permute-start(bf16[2,512]{1,0:T(2,128)(2,1)S(1)} %slice.1952), channel_id=1, source_target_pairs={{0,8},{8,16},{16,24},{24,32},{32,40},{40,48},{48,56},{56,64},{64,7... | collective-permute-start | bytes 6152 | tf_op jit(solution)/shard_map/ppermute | solution.py:13
  16.5 11.3 %all-to-all-start = ((bf16[48,8,512]{2,0,1:T(8,128)(2,1)}), bf16[48,8,512]{2,0,1:T(8,128)(2,1)S(1)}, u32[]{:S(2)}, u32[]{:S(2)}) async-start(bf16[48,8,512]{2,0,1:T(8,128)(2,1)} %bitcast.571), calls=%async_computation | async-start | bytes 786432 | tf_op jit(solution)/shard_map/all_to_all | solution.py:77
  21.2 73.2 %all-gather.2.cloned.1.call-start = ((), (), s32[]{:S(2)}) async-start(), calls=%async_computation.1 | async-start | bytes 6684672 | tf_op jit(solution)/shard_map/all_gather | solution.py:94
  22.7 71.7 %copy-start.3 = (f32[1,1,512]{2,1,0:T(1,128)}, f32[1,1,512]{2,1,0:T(1,128)S(1)}, u32[]{:S(2)}) copy-start(f32[1,1,512]{2,1,0:T(1,128)S(1)} %get-tuple-element.1060) | copy-start | bytes 6148
  22.7 71.7 %copy-start.4 = (f32[1,1,512]{2,1,0:T(1,128)}, f32[1,1,512]{2,1,0:T(1,128)S(1)}, u32[]{:S(2)}) copy-start(f32[1,1,512]{2,1,0:T(1,128)S(1)} %get-tuple-element.1061) | copy-start | bytes 6148
  22.7 71.7 %copy-start.5 = (f32[1,1,512]{2,1,0:T(1,128)}, f32[1,1,512]{2,1,0:T(1,128)S(1)}, u32[]{:S(2)}) copy-start(f32[1,1,512]{2,1,0:T(1,128)S(1)} %get-tuple-element.1062) | copy-start | bytes 6148
  30.0 64.4 %copy-start.2 = (f32[384,512]{1,0:T(8,128)}, f32[384,512]{1,0:T(8,128)S(1)}, u32[]{:S(2)}) copy-start(f32[384,512]{1,0:T(8,128)S(1)} %get-tuple-element.1055) | copy-start | bytes 2359300
  30.7 8.0 %collective-permute-start.2 = (bf16[2,512]{1,0:T(2,128)(2,1)S(1)}, bf16[2,512]{1,0:T(2,128)(2,1)S(1)}, u32[]{:S(2)}, u32[]{:S(2)}) collective-permute-start(bf16[2,512]{1,0:T(2,128)(2,1)S(1)} %slice.1957), channel_id=1, source_target_pairs={{0,8},{8,16},{16,24},{24,32},{32,40},{40,48},{48,56},{56,64},{64,7... | collective-permute-start | bytes 6152 | tf_op jit(solution)/shard_map/ppermute | solution.py:13
  36.7 4.2 collective-permute-start.4
  43.5 643.9 %collective-permute-start = (f32[2,512]{1,0:T(2,128)}, f32[2,512]{1,0:T(2,128)}, u32[]{:S(2)}, u32[]{:S(2)}) collective-permute-start(f32[2,512]{1,0:T(2,128)} %slice.2078), channel_id=1, source_target_pairs={{8,0},{16,8},{24,16},{32,24},{40,32},{48,40},{56,48},{64,56},{72,6... | collective-permute-start | bytes 12296 | tf_op jit(solution)/shard_map/ppermute | solution.py:13
  94.4 589.1 %copy-start = (f32[386,512]{1,0:T(8,128)S(1)}, f32[386,512]{1,0:T(8,128)}, u32[]{:S(2)}) copy-start(f32[386,512]{1,0:T(8,128)} %maximum_convert_fusion.1) | copy-start | bytes 2371588
  94.4 589.1 %copy-start.1 = (f32[386,512]{1,0:T(8,128)S(1)}, f32[386,512]{1,0:T(8,128)}, u32[]{:S(2)}) copy-start(f32[386,512]{1,0:T(8,128)} %maximum_convert_fusion.2) | copy-start | bytes 2371588
  94.4 589.1 %copy-start.6 = (f32[1,1,512]{2,1,0:T(1,128)S(1)}, f32[1,1,512]{2,1,0:T(1,128)}, u32[]{:S(2)}) copy-start(f32[1,1,512]{2,1,0:T(1,128)} %get-tuple-element.1056) | copy-start | bytes 6148
  94.4 589.1 %copy-start.7 = (f32[1,1,512]{2,1,0:T(1,128)S(1)}, f32[1,1,512]{2,1,0:T(1,128)}, u32[]{:S(2)}) copy-start(f32[1,1,512]{2,1,0:T(1,128)} %get-tuple-element.1063) | copy-start | bytes 6148
  94.4 589.1 %copy-start.8 = (f32[1,1,512]{2,1,0:T(1,128)S(1)}, f32[1,1,512]{2,1,0:T(1,128)}, u32[]{:S(2)}) copy-start(f32[1,1,512]{2,1,0:T(1,128)} %get-tuple-element.1064) | copy-start | bytes 6148
  94.4 589.1 %copy-start.9 = (f32[1,1,512]{2,1,0:T(1,128)S(1)}, f32[1,1,512]{2,1,0:T(1,128)}, u32[]{:S(2)}) copy-start(f32[1,1,512]{2,1,0:T(1,128)} %get-tuple-element.1057) | copy-start | bytes 6148
  94.4 589.1 %copy-start.10 = (f32[1,1,512]{2,1,0:T(1,128)S(1)}, f32[1,1,512]{2,1,0:T(1,128)}, u32[]{:S(2)}) copy-start(f32[1,1,512]{2,1,0:T(1,128)} %get-tuple-element.1058) | copy-start | bytes 6148
  94.4 589.1 %copy-start.11 = (f32[1,1,512]{2,1,0:T(1,128)S(1)}, f32[1,1,512]{2,1,0:T(1,128)}, u32[]{:S(2)}) copy-start(f32[1,1,512]{2,1,0:T(1,128)} %get-tuple-element.1059) | copy-start | bytes 6148
  685.2 6.9 collective-permute-start.5
  690.2 6.4 collective-permute-start.3
Sparse Core Ops, SparseCore 0:
  30.1 64.1 all-gather.1
where the time goes:
time: 712 us; the launch traced here: 705 us
  local copies, waits for them, and re-layouts  416 us (58%)
  matrix products  165 us (23%)
  waiting for transfers between devices  56.2 us (8%)
  other arithmetic  26.8 us (4%)
  starting transfers between devices  25.2 us (4%)
  between operations  14.4 us (2%)
    reshape x1, local copies, waits for them, and re-layouts, toeplitz_tiles(): tiled[:, :tile_rows * (width_k + tile_rows - 1)]  209 us
    cond x48, matrix products  161 us
    slice x101, local copies, waits for them, and re-layouts, cross_terms(): pieces[lowest + offset:highest + offset]  87 us
    cond x2, local copies, waits for them, and re-layouts  49.1 us
    all_gather x1, waiting for transfers between devices, body(): piece = lax.all_gather(grad_conv, 'ctx', axis=0, tiled=True)  48.6 us
    slice x1, local copies, waits for them, and re-layouts, toeplitz_tiles(): tiled[:, :tile_rows * (width_k + tile_rows - 1)]  35.7 us
    ppermute x6, starting transfers between devices, shifted(): return lax.ppermute(array, axis, pairs)  20.5 us
    another operation x1, local copies, waits for them, and re-layouts, toeplitz_tiles(): tiled = jnp.tile(padded, (1, tile_rows))  17.2 us
  transfers between devices with their start and end apart: 8, of which 3 were waited for; matrix products, arithmetic and copies ran while one was open for 86% of the time, Pallas kernels for 0%

commit v1 on v0

--- a/solution.py
+++ b/solution.py
@@ -91,7 +91,9 @@
     grad_qfeat = upstream_f * saved_conv.astype(jnp.float32)
     grad_conv = (upstream_f * query_feat).astype(jnp.bfloat16)
     empty = jnp.zeros((block_rows, channels), jnp.float32)
-    piece = lax.all_gather(grad_conv, "ctx", axis=0, tiled=True)
+    piece = jnp.concatenate(
+        lax.all_to_all(jnp.stack([grad_conv] * lax.axis_size("ctx")), "ctx", 0, 0), axis=0
+    )
     piece_start = jnp.int32(0)
     grad_mix = lax.cond(
         piece_start + piece.shape[0] > own_start,

time: 712 us -> 782 us (1.098)
  local copies, waits for them, and re-layouts: 416 us -> 458 us
  waiting for transfers between devices: 56.2 us -> 87.7 us
  between operations: 14.4 us -> 1.07 us
    all_to_all x0 -> x1, waiting for transfers between devices: none -> 62.8 us  [body(): lax.all_to_all(jnp.stack([grad_conv] * lax.axis_size('ctx')), 'ctx', 0, 0)]
    all_gather x1 -> x0, waiting for transfers between devices: 48.6 us -> none  [body(): piece = lax.all_gather(grad_conv, 'ctx', axis=0, tiled=True)]
    cond x2 -> x34, local copies, waits for them, and re-layouts: 49.1 us -> 78 us
    ppermute x6, waiting for transfers between devices: 3.51 us -> 20.9 us  [shifted(): return lax.ppermute(array, axis, pairs)]
    another operation x1 -> x3, local copies, waits for them, and re-layouts: 8.87 us -> 23 us  [the longest x1 10.5 us: cross_terms(): pieces = source.reshape(src_tiles, tile_rows, groups, GSIZE)]
    slice x101 -> x37, local copies, waits for them, and re-layouts: 87 us -> 85.9 us  [cross_terms(): pieces[lowest + offset:highest + offset]]
  transfers between devices with their start and end apart: 8 -> 8, of which waited for: 3 -> 5; matrix products, arithmetic and copies ran while one was open for 86% -> 83% of each run, Pallas kernels for 0% -> 0%
where the time goes in v1:
time: 782 us; the launch traced here: 770 us
  local copies, waits for them, and re-layouts  458 us (59%)
  matrix products  165 us (21%)
  waiting for transfers between devices  87.7 us (11%)
  starting transfers between devices  32.8 us (4%)
  other arithmetic  24.9 us (3%)
    reshape x1, local copies, waits for them, and re-layouts, toeplitz_tiles(): tiled[:, :tile_rows * (width_k + tile_rows - 1)]  209 us
    cond x48, matrix products  161 us
    slice x37, local copies, waits for them, and re-layouts, cross_terms(): pieces[lowest + offset:highest + offset]  85.9 us
    cond x34, local copies, waits for them, and re-layouts  78 us
    all_to_all x1, waiting for transfers between devices, body(): lax.all_to_all(jnp.stack([grad_conv] * lax.axis_size('ctx')), 'ctx', 0, 0)  62.8 us
    slice x1, local copies, waits for them, and re-layouts, toeplitz_tiles(): tiled[:, :tile_rows * (width_k + tile_rows - 1)]  35.7 us
    ppermute x6, waiting for transfers between devices, shifted(): return lax.ppermute(array, axis, pairs)  20.9 us
    ppermute x6, starting transfers between devices, shifted(): return lax.ppermute(array, axis, pairs)  20.4 us
  transfers between devices with their start and end apart: 8, of which 5 were waited for; matrix products, arithmetic and copies ran while one was open for 83% of the time, Pallas kernels for 0%

profile of v1, /device:TPU:1, one launch (start us, length us, event | category | flops | bytes accessed | tf_op | source)
XLA Modules:
  0.0 770.4 jit_solution(5871434824340911095)
XLA Ops:
  1.3 6.9 collective-permute-start.1
  10.0 4.6 all-to-all-start
  17.3 4.1 all-to-all-done
  22.9 3.4 stack.2
  26.4 7.8 %all-to-all-start.1 = ((bf16[16,384,512]{1,2,0:T(8,128)(2,1)}), bf16[16,384,512]{1,2,0:T(8,128)(2,1)}, u32[]{:S(2)}, u32[]{:S(2)}) async-start(bf16[16,384,512]{1,2,0:T(8,128)(2,1)} %stack.2), calls=%async_computation.1 | async-start | bytes 12582912 | tf_op jit(solution)/shard_map/all_to_all | solution.py:95
  34.8 5.0 collective-permute-start.4
  42.6 17.4 %collective-permute-done.4 = bf16[2,512]{1,0:T(2,128)(2,1)S(1)} collective-permute-done((bf16[2,512]{1,0:T(2,128)(2,1)S(1)}, bf16[2,512]{1,0:T(2,128)(2,1)S(1)}, u32[]{:S(2)}, u32[]{:S(2)}) %collective-permute-start.4) | collective-permute-done | bytes 2080 | tf_op jit(solution)/shard_map/ppermute | solution.py:13
  66.6 62.8 %all-to-all-done.1 = bf16[16,384,512]{1,2,0:T(8,128)(2,1)} async-done(((bf16[16,384,512]{1,2,0:T(8,128)(2,1)}), bf16[16,384,512]{1,2,0:T(8,128)(2,1)}, u32[]{:S(2)}, u32[]{:S(2)}) %all-to-all-start.1) | async-done | bytes 6291488 | tf_op jit(solution)/shard_map/all_to_all | solution.py:95
  129.4 627.2 %conditional.1 = (f32[384,512]{1,0:T(8,128)}) conditional(s32[]{:T(128)} %convert_element_type.43, () %tuple.355, (bf16[32,6144]{1,0:T(8,128)(2,1)}, s32[]{:T(128)}, bf16[16,384,512]{1,2,0:T(8,128)(2,1)}) %tuple.356), branch_computations={%region_0.1_spmd, %region_1.2_spmd} | conditional | flops 2425290752 | bytes 645726144 | solution.py:98
  130.8 17.2 %tile.1 = bf16[32,128,6528]{2,1,0:T(8,128)(2,1)} broadcast(bf16[32,6528]{1,0:T(8,128)(2,1)S(1)} %concatenate.114), dimensions={0,2} | broadcast | bytes 53895168 | tf_op jit(solution)/shard_map/cond/branch_1_fun/tile | solution.py:37
  148.0 49.0 %copy.232 = bf16[4,8,128,6528]{3,1,2,0:T(8,128)(2,1)} copy(bf16[4,8,128,6528]{3,2,1,0:T(8,128)(2,1)} %bitcast.512) | data formatting | bytes 106954752 | tf_op jit(solution)/shard_map/cond
  197.0 35.7 %slice.1877 = bf16[32,835456]{1,0:T(8,128)(2,1)} slice(bf16[32,835584]{1,0:T(8,128)(2,1)} %bitcast.513), slice={[0:32], [0:835456]} | slice | bytes 106938368 | tf_op jit(solution)/shard_map/cond/branch_1_fun/slice | solution.py:38
  232.7 209.0 %reshape.2065 = bf16[32,128,6527]{2,1,0:T(8,128)(2,1)} reshape(bf16[32,835456]{1,0:T(8,128)(2,1)} %slice.1877) | data formatting | bytes 106938368 | tf_op jit(solution)/shard_map/cond/branch_1_fun/reshape | solution.py:38
  441.8 9.1 %copy.92 = bf16[16,384,512]{1,0,2:T(8,128)(2,1)} copy(bf16[16,384,512]{1,2,0:T(8,128)(2,1)} %get-tuple-element.987) | data formatting | bytes 12582912 | tf_op jit(solution)/shard_map
  450.9 10.5 %reshape_reshape.3 = bf16[48,128,32,16]{1,0,3,2:T(8,128)(2,1)} reshape(bf16[16,384,512]{1,0,2:T(8,128)(2,1)} %copy.92) | data formatting | bytes 12582912 | tf_op jit(solution)/shard_map/cond/branch_1_fun/reshape;reshape | solution.py:53
  470.9 5.5 fusion.131
  479.5 3.4 fusion.5
  483.0 15.1 %fusion.132 = (bf16[3,128,32,16]{1,0,3,2:T(4,128)(2,1)}, bf16[3,128,32,16]{1,0,3,2:T(4,128)(2,1)S(1)}, bf16[3,128,32,16]{1,0,3,2:T(4,128)(2,1)S(1)}, bf16[3,128,...) fusion(bf16[48,128,32,16]{1,0,3,2:T(8,128)(2,1)} %reshape_reshape.3), kind=kLoop, calls=%fused_computation.210 | loop fusion | bytes 14942208 | tf_op jit(solution)/shard_map/cond/branch_1_fun/slice | solution.py:63
  498.1 3.4 fusion.7
  501.6 3.4 fusion.9
  508.2 3.4 fusion.11
  512.7 3.4 fusion.13
  517.2 3.4 fusion.15
  523.8 3.4 fusion.17
  528.3 3.4 fusion.19
  532.8 3.4 fusion.21
  539.3 3.4 fusion.23
  543.9 3.4 fusion.25
  548.4 3.4 fusion.27
  555.1 3.4 fusion.29
  559.6 3.4 fusion.31
  564.1 3.4 fusion.33
  570.7 3.4 fusion.35
  575.2 3.4 fusion.37
  579.7 3.4 fusion.39
  590.7 3.4 fusion.43
  595.3 3.4 fusion.45
  601.9 3.4 fusion.47
  606.4 3.4 fusion.49
  610.9 3.4 fusion.51
  617.6 3.4 fusion.53
  622.2 3.5 fusion.55
  626.7 3.4 fusion.57
  633.3 3.4 fusion.59
  636.7 9.6 %fusion.133 = (bf16[3,128,32,16]{1,0,3,2:T(4,128)(2,1)}, bf16[3,128,32,16]{1,0,3,2:T(4,128)(2,1)S(1)}, bf16[3,128,32,16]{1,0,3,2:T(4,128)(2,1)S(1)}, bf16[3,128,...) fusion(bf16[48,128,32,16]{1,0,3,2:T(8,128)(2,1)} %reshape_reshape.3), kind=kLoop, calls=%fused_computation.211 | loop fusion | bytes 8650752 | tf_op jit(solution)/shard_map/cond/branch_1_fun/slice | solution.py:63
  646.4 3.4 fusion.61
  649.8 3.4 fusion.63
  656.4 3.4 fusion.65
  660.9 3.4 fusion.67
  665.4 3.4 fusion.69
  672.0 3.4 fusion.71
  676.5 3.4 fusion.73
  681.0 3.4 fusion.75
  687.9 3.4 fusion.77
  692.5 3.4 fusion.79
  697.0 3.4 fusion.81
  703.5 3.4 fusion.83
  708.1 3.4 fusion.85
  712.6 3.4 fusion.87
  719.1 3.4 fusion.89
  723.6 3.4 fusion.91
  728.1 3.4 fusion.93
  737.2 12.7 %bitcast_add_fusion = f32[3,128,32,16]{1,3,2,0:T(8,128)S(1)} fusion(f32[3,128,32,16]{1,3,2,0:T(8,128)S(1)} %fusion.100, f32[32,128,3,16]{1,3,2,0:T(8,128)} %bitcast.516, f32[32,128,3,16]{1,3,2,0:T(8,128)} %bitcast.517, f32[32,128,3,16]{1,3,2,0:T(8,128)} %bitcast.518, f32[32,128,3,16]{1,3,2,0:T(8,128)} %bitcast.519, f32[32,128,3,16]{1,3,2,0:T(8,128)} %bitcast.520, ...), kind=kLoop, calls=%fused_computation.104 | loop fusion | flops 9043968 | bytes 37748736 | tf_op jit(solution)/shard_map/cond/branch_1_fun/add | solution.py:66
  765.8 3.4 collective-permute-done.5
  (131 shorter events, 130.2 us)
Async XLA Ops:
  1.3 14.8 %collective-permute-start.1 = (bf16[2,512]{1,0:T(2,128)(2,1)S(1)}, bf16[2,512]{1,0:T(2,128)(2,1)S(1)}, u32[]{:S(2)}, u32[]{:S(2)}) collective-permute-start(bf16[2,512]{1,0:T(2,128)(2,1)S(1)} %slice.1854), channel_id=1, source_target_pairs={{0,8},{8,16},{16,24},{24,32},{32,40},{40,48},{48,56},{56,64},{64,7... | collective-permute-start | bytes 6152 | tf_op jit(solution)/shard_map/ppermute | solution.py:13
  10.0 11.3 %all-to-all-start = ((bf16[48,8,512]{2,0,1:T(8,128)(2,1)}), bf16[48,8,512]{2,0,1:T(8,128)(2,1)S(1)}, u32[]{:S(2)}, u32[]{:S(2)}) async-start(bf16[48,8,512]{2,0,1:T(8,128)(2,1)} %bitcast.511), calls=%async_computation | async-start | bytes 786432 | tf_op jit(solution)/shard_map/all_to_all | solution.py:77
  16.1 113.3 %copy-start.4 = (f32[1,1,512]{2,1,0:T(1,128)}, f32[1,1,512]{2,1,0:T(1,128)S(1)}, u32[]{:S(2)}) copy-start(f32[1,1,512]{2,1,0:T(1,128)S(1)} %get-tuple-element.1054) | copy-start | bytes 6148
  16.1 113.3 %copy-start.5 = (f32[1,1,512]{2,1,0:T(1,128)}, f32[1,1,512]{2,1,0:T(1,128)S(1)}, u32[]{:S(2)}) copy-start(f32[1,1,512]{2,1,0:T(1,128)S(1)} %get-tuple-element.1055) | copy-start | bytes 6148
  16.1 113.3 %copy-start.6 = (f32[1,1,512]{2,1,0:T(1,128)}, f32[1,1,512]{2,1,0:T(1,128)S(1)}, u32[]{:S(2)}) copy-start(f32[1,1,512]{2,1,0:T(1,128)S(1)} %get-tuple-element.1056) | copy-start | bytes 6148
  22.7 106.7 %copy-start.2 = (f32[384,512]{1,0:T(8,128)}, f32[384,512]{1,0:T(8,128)S(1)}, u32[]{:S(2)}) copy-start(f32[384,512]{1,0:T(8,128)S(1)} %get-tuple-element.1049) | copy-start | bytes 2359300
  26.4 103.0 %all-to-all-start.1 = ((bf16[16,384,512]{1,2,0:T(8,128)(2,1)}), bf16[16,384,512]{1,2,0:T(8,128)(2,1)}, u32[]{:S(2)}, u32[]{:S(2)}) async-start(bf16[16,384,512]{1,2,0:T(8,128)(2,1)} %stack.2), calls=%async_computation.1 | async-start | bytes 12582912 | tf_op jit(solution)/shard_map/all_to_all | solution.py:95
  34.8 25.2 %collective-permute-start.4 = (bf16[2,512]{1,0:T(2,128)(2,1)S(1)}, bf16[2,512]{1,0:T(2,128)(2,1)S(1)}, u32[]{:S(2)}, u32[]{:S(2)}) collective-permute-start(bf16[2,512]{1,0:T(2,128)(2,1)S(1)} %slice.1870), channel_id=1, source_target_pairs={{0,8},{8,16},{16,24},{24,32},{32,40},{40,48},{48,56},{56,64},{64,7... | collective-permute-start | bytes 6152 | tf_op jit(solution)/shard_map/ppermute | solution.py:13
  40.6 21.4 %collective-permute-start.2 = (bf16[2,512]{1,0:T(2,128)(2,1)S(1)}, bf16[2,512]{1,0:T(2,128)(2,1)S(1)}, u32[]{:S(2)}, u32[]{:S(2)}) collective-permute-start(bf16[2,512]{1,0:T(2,128)(2,1)S(1)} %slice.1859), channel_id=1, source_target_pairs={{0,8},{8,16},{16,24},{24,32},{32,40},{40,48},{48,56},{56,64},{64,7... | collective-permute-start | bytes 6152 | tf_op jit(solution)/shard_map/ppermute | solution.py:13
  64.7 696.4 %collective-permute-start = (f32[2,512]{1,0:T(2,128)}, f32[2,512]{1,0:T(2,128)}, u32[]{:S(2)}, u32[]{:S(2)}) collective-permute-start(f32[2,512]{1,0:T(2,128)} %slice.1964), channel_id=1, source_target_pairs={{8,0},{16,8},{24,16},{32,24},{40,32},{48,40},{56,48},{64,56},{72,6... | collective-permute-start | bytes 12296 | tf_op jit(solution)/shard_map/ppermute | solution.py:13
  129.3 627.3 %copy-start = (f32[386,512]{1,0:T(8,128)S(1)}, f32[386,512]{1,0:T(8,128)}, u32[]{:S(2)}) copy-start(f32[386,512]{1,0:T(8,128)} %maximum_convert_fusion.2) | copy-start | bytes 2371588
  129.3 627.3 %copy-start.1 = (f32[386,512]{1,0:T(8,128)S(1)}, f32[386,512]{1,0:T(8,128)}, u32[]{:S(2)}) copy-start(f32[386,512]{1,0:T(8,128)} %maximum_convert_fusion.1) | copy-start | bytes 2371588
  129.3 627.3 %copy-start.7 = (f32[1,1,512]{2,1,0:T(1,128)S(1)}, f32[1,1,512]{2,1,0:T(1,128)}, u32[]{:S(2)}) copy-start(f32[1,1,512]{2,1,0:T(1,128)} %get-tuple-element.1051) | copy-start | bytes 6148
  129.4 627.3 %copy-start.8 = (f32[1,1,512]{2,1,0:T(1,128)S(1)}, f32[1,1,512]{2,1,0:T(1,128)}, u32[]{:S(2)}) copy-start(f32[1,1,512]{2,1,0:T(1,128)} %get-tuple-element.1052) | copy-start | bytes 6148
  129.4 627.3 %copy-start.9 = (f32[1,1,512]{2,1,0:T(1,128)S(1)}, f32[1,1,512]{2,1,0:T(1,128)}, u32[]{:S(2)}) copy-start(f32[1,1,512]{2,1,0:T(1,128)} %get-tuple-element.1053) | copy-start | bytes 6148
  129.4 627.3 %copy-start.10 = (f32[1,1,512]{2,1,0:T(1,128)S(1)}, f32[1,1,512]{2,1,0:T(1,128)}, u32[]{:S(2)}) copy-start(f32[1,1,512]{2,1,0:T(1,128)} %get-tuple-element.1050) | copy-start | bytes 6148
  129.4 627.3 %copy-start.11 = (f32[1,1,512]{2,1,0:T(1,128)S(1)}, f32[1,1,512]{2,1,0:T(1,128)}, u32[]{:S(2)}) copy-start(f32[1,1,512]{2,1,0:T(1,128)} %get-tuple-element.1057) | copy-start | bytes 6148
  129.4 627.3 %copy-start.12 = (f32[1,1,512]{2,1,0:T(1,128)S(1)}, f32[1,1,512]{2,1,0:T(1,128)}, u32[]{:S(2)}) copy-start(f32[1,1,512]{2,1,0:T(1,128)} %get-tuple-element.1058) | copy-start | bytes 6148
  129.4 631.6 %copy-start.3 = (f32[384,512]{1,0:T(8,128)S(1)}, f32[384,512]{1,0:T(8,128)}, u32[]{:S(2)}) copy-start(f32[384,512]{1,0:T(8,128)} %copy-done.2) | copy-start | bytes 2359300
  758.3 6.4 collective-permute-start.3
  762.8 6.4 collective-permute-start.5
